TPU v7x, 512 devices: a whole 4x8x8 slice. The times are simulated.
512 devices in a mesh: hrow: 16 (over y_lo, z), hcol: 32 (over x, y_hi, core).
Axes of the slice: x: 4, y: 8 (y_hi: 4, y_lo: 2; y = y_hi * 2 + y_lo), z: 8, core: 2. Of those that a mesh axis runs over, the one named last changes fastest.
Arguments:
- expect: bfloat16 [2, 1024, 102400], P(None, 'hrow', 'hcol'), may hold values from -6 to 6
- distrib: bfloat16 [2, 1024, 102400], P(None, 'hrow', 'hcol'), may hold values from -0.0024414062 to 0.0024414062
- direct: float32 [2, 2, 1024], P(None, None, 'hcol'), may hold values from -4 to 4
- pair_index: int32 [4, 2], replicated, may hold values from 0 to 1
Outputs:
- jacobian: float32 [4, 1024, 1024], P(None, 'hrow', 'hcol')
Inputs may be any that keep to these rules, and one draw needn't show every extreme that they name: `pair_index`: column 0 of each row names a shock and column 1 an output; pairs may repeat.
All inputs are finite; a program needn't handle non-finite values.
Results may differ from a plain program's by a relative error of at most 0.0003.
Values may be sent and summed in bfloat16 or wider, within the bound.
A program may use at most 64 MiB of HBM per device.

v0:
```python
import jax
import jax.numpy as jnp
from jax import lax
from jax.sharding import PartitionSpec as P


def from_behind(block, axis, distance):
    devices = range(lax.axis_size(axis))
    route = [(i - distance, i) for i in devices if i - distance in devices]
    return lax.ppermute(block, axis, route)


def diagonal_sums(values):
    row_count = values.shape[1]
    col_count = values.shape[2]
    offset = 1
    while offset < min(row_count, col_count):
        padded = jnp.pad(values, ((0, 0), (offset, 0), (offset, 0)))
        values = values + padded[:, :row_count, :col_count]
        offset = offset * 2
    return values


def shift_down(values, amount):
    if amount == 0:
        return values
    width_rows = values.shape[1]
    filler = jnp.zeros((values.shape[0], amount), values.dtype)
    return jnp.concatenate([filler, values[:, : width_rows - amount]], axis=1)


def shards(expect, distrib, direct, pair_index):
    row_devices = lax.axis_size("hrow")
    col_devices = lax.axis_size("hcol")
    stride = col_devices // row_devices
    output_count, row_count, _ = expect.shape
    shock_count = distrib.shape[0]
    horizon_all = distrib.shape[1] * row_devices
    col_count = horizon_all // col_devices
    pair_count = pair_index.shape[0]
    partial_tiles = jnp.einsum(
        "orn,scn->osrc",
        expect,
        lax.all_gather(distrib, "hrow", axis=1, tiled=True),
        preferred_element_type=jnp.float32,
    )
    products = lax.psum_scatter(partial_tiles, "hcol", scatter_dimension=3, tiled=True)
    shock_pick = (pair_index[:, 0][:, None] == jnp.arange(shock_count)[None, :]).astype(jnp.float32)
    output_pick = (pair_index[:, 1][:, None] == jnp.arange(output_count)[None, :]).astype(
        jnp.float32
    )
    weights = output_pick[:, :, None] * shock_pick[:, None, :]
    fake_news = jnp.sum(weights[:, :, :, None, None] * products[None], axis=(1, 2))
    direct_pick = jnp.sum(
        shock_pick[:, :, None, None] * output_pick[:, None, :, None] * direct[None], axis=(1, 2)
    )
    top_first = jnp.where(lax.axis_index("hrow") == 0, direct_pick, jnp.zeros_like(direct_pick))
    fake_news = fake_news.at[:, 0, :].add(top_first)
    within = diagonal_sums(fake_news)
    last_col = within[:, :, col_count - 1]
    incoming = jnp.zeros((pair_count, row_count), jnp.float32)
    for offset in range(1, stride + 1):
        shifted = from_behind(last_col, "hcol", offset)
        incoming = incoming + shift_down(shifted, (offset - 1) * col_count)
    padded_in = jnp.concatenate([jnp.zeros((pair_count, 1), jnp.float32), incoming], axis=1)
    band_last = within[:, row_count - 1, :] + jnp.flip(
        padded_in[:, row_count - col_count : row_count], axis=1
    )

    def advance(counter, received):
        moved = from_behind(received, "hcol", stride)
        return from_behind(band_last + moved, "hrow", 1)

    prev_band = lax.fori_loop(0, row_devices - 1, advance, jnp.zeros_like(band_last))
    blocks = [prev_band]
    for offset in range(1, stride + 1):
        blocks.insert(0, from_behind(prev_band, "hcol", offset))
    window = jnp.concatenate(blocks, axis=1)
    top_rim = window[:, row_count - 1 : row_count + col_count - 1]
    left_rim = incoming[:, : row_count - 1] + jnp.flip(window[:, : row_count - 1], axis=1)
    injected = jnp.zeros((pair_count, row_count, col_count), jnp.float32)
    injected = injected.at[:, 0, :].set(top_rim)
    injected = injected.at[:, 1:, 0].set(left_rim)
    return within + diagonal_sums(injected)


def solution(mesh):
    placed = (P(None, "hrow", "hcol"), P(None, "hrow", "hcol"), P(None, None, "hcol"), P())
    return jax.shard_map(
        shards, mesh=mesh, in_specs=placed, out_specs=P(None, "hrow", "hcol"), check_vma=False
    )
```

profile of v0, /device:TPU:14, one launch (start us, length us, event | category | flops | bytes accessed | tf_op | source)
XLA Modules:
  0.0 734.6 jit_solution(15291740475848407517)
XLA Ops:
  7.3 157.6 %all-gather.2.cloned.1.call-done = bf16[2,1024,3200]{2,1,0:T(8,128)(2,1)} async-done(((bf16[2,64,3200]{2,1,0:T(8,128)(2,1)}), bf16[2,1024,3200]{2,1,0:T(8,128)(2,1)}) %all-gather.2.cloned.1.call-update) | async-done | bytes 13107216 | tf_op jit(solution)/shard_map/all_gather | solution.py:44
  164.9 9.0 %fusion.2 = f32[2,2,64,1024]{3,2,0,1:T(8,128)S(1)} fusion(bf16[2,1024,3200]{2,1,0:T(8,128)(2,1)} %all-gather.2.cloned.1.call-done, bf16[2,64,3200]{2,1,0:T(8,128)(2,1)S(1)} %copy-done), kind=kOutput, calls=%fused_computation.2 | convolution fusion | flops 1677721600 | bytes 14974976 | tf_op jit(solution)/shard_map/orn,scn->osrc/dot_general | solution.py:41
  178.6 277.5 %all-reduce.15.cloned.1.call-done = f32[2,2,64,1024]{2,1,0,3:T(2,128)} async-done(((f32[2,2,64,1024]{2,1,0,3:T(2,128)}), f32[2,2,64,1024]{2,1,0,3:T(2,128)}) %all-reduce.15.cloned.1.call-update) | async-done | bytes 1048592
  457.6 7.7 %collective-permute-start.3 = (f32[4,64]{1,0:T(4,128)S(1)}, f32[4,64]{1,0:T(4,128)S(1)}, u32[]{:S(2)}, u32[]{:S(2)}) collective-permute-start(f32[4,64]{1,0:T(4,128)S(1)} %bitcast.30), channel_id=1, source_target_pairs={{0,2},{1,3},{2,4},{3,5},{4,6},{5,7},{6,8},{7,9},{8,10},{9,11},{10,... | collective-permute-start | bytes 3080 | tf_op jit(solution)/shard_map/ppermute | solution.py:10
  473.5 241.6 %while.13 = (s32[]{:T(128)}, f32[4,32]{1,0:T(4,128)S(1)}, f32[4,32]{1,0:T(4,128)S(1)}, s32[]{:T(128)}) while((s32[]{:T(128)}, f32[4,32]{1,0:T(4,128)S(1)}, f32[4,32]{1,0:T(4,128)S(1)}, s32[]{:T(128)}) %tuple.35), condition=%wide.region_4.5_spmd, body=%wide.region_3.4_spmd.sunk | while | flops 130 | bytes 5765 | solution.py:74
  500.7 5.7 collective-permute-done.1
  516.8 5.7 collective-permute-done.1
  525.2 5.7 collective-permute-done
  532.8 5.7 collective-permute-done.1
  540.4 6.6 collective-permute-done
  556.4 6.6 collective-permute-done
  564.9 5.7 collective-permute-done.1
  572.5 6.6 collective-permute-done
  581.0 5.7 collective-permute-done.1
  588.6 6.6 collective-permute-done
  597.0 5.7 collective-permute-done.1
  604.6 6.6 collective-permute-done
  613.1 5.7 collective-permute-done.1
  620.7 6.6 collective-permute-done
  636.7 6.6 collective-permute-done
  652.8 6.6 collective-permute-done
  668.8 6.6 collective-permute-done
  684.9 6.6 collective-permute-done
  701.0 6.6 collective-permute-done
  (113 shorter events, 150.9 us)
Async XLA Ops:
  6.5 158.3 %all-gather.2.cloned.1.call-start = ((), (), s32[]{:S(2)}) async-start(), calls=%async_computation | async-start | bytes 13926400 | tf_op jit(solution)/shard_map/all_gather | solution.py:44
  7.3 448.8 %all-reduce.15.cloned.1.call-start = ((), (), s32[]{:S(2)}) async-start(), calls=%async_computation.1 | async-start | bytes 4194304
  457.6 10.9 %collective-permute-start.3 = (f32[4,64]{1,0:T(4,128)S(1)}, f32[4,64]{1,0:T(4,128)S(1)}, u32[]{:S(2)}, u32[]{:S(2)}) collective-permute-start(f32[4,64]{1,0:T(4,128)S(1)} %bitcast.30), channel_id=1, source_target_pairs={{0,2},{1,3},{2,4},{3,5},{4,6},{5,7},{6,8},{7,9},{8,10},{9,11},{10,... | collective-permute-start | bytes 3080 | tf_op jit(solution)/shard_map/ppermute | solution.py:10
  465.3 7.9 %collective-permute-start.2 = (f32[4,64]{1,0:T(4,128)S(1)}, f32[4,64]{1,0:T(4,128)S(1)}, u32[]{:S(2)}, u32[]{:S(2)}) collective-permute-start(f32[4,64]{1,0:T(4,128)S(1)} %bitcast.31), channel_id=1, source_target_pairs={{0,1},{1,2},{2,3},{3,4},{4,5},{5,6},{6,7},{7,8},{8,9},{9,10},{10,1... | collective-permute-start | bytes 3080 | tf_op jit(solution)/shard_map/ppermute | solution.py:10
  473.5 8.5 %collective-permute-start = (f32[4,32]{1,0:T(4,128)S(1)}, f32[4,32]{1,0:T(4,128)S(1)}, u32[]{:S(2)}, u32[]{:S(2)}) collective-permute-start(f32[4,32]{1,0:T(4,128)S(1)} %get-tuple-element.101), channel_id=1, source_target_pairs={{0,2},{1,3},{2,4},{3,5},{4,6},{5,7},{6,8},{7,9},{8,10},{9,11},{10,... | collective-permute-start | bytes 1544 | tf_op jit(solution)/shard_map/while/body/eval_jaxpr/ppermute | solution.py:10
  482.0 8.3 %collective-permute-start.1 = (f32[4,32]{1,0:T(4,128)S(1)}, f32[4,32]{1,0:T(4,128)S(1)}, u32[]{:S(2)}, u32[]{:S(2)}) collective-permute-start(f32[4,32]{1,0:T(4,128)S(1)} %add.124), channel_id=1, source_target_pairs={{0,32},{32,64},{64,96},{96,128},{128,160},{160,192},{192,224},{224... | collective-permute-start | bytes 1544 | tf_op jit(solution)/shard_map/while/body/eval_jaxpr/ppermute | solution.py:10
  490.3 8.5 %collective-permute-start = (f32[4,32]{1,0:T(4,128)S(1)}, f32[4,32]{1,0:T(4,128)S(1)}, u32[]{:S(2)}, u32[]{:S(2)}) collective-permute-start(f32[4,32]{1,0:T(4,128)S(1)} %get-tuple-element.101), channel_id=1, source_target_pairs={{0,2},{1,3},{2,4},{3,5},{4,6},{5,7},{6,8},{7,9},{8,10},{9,11},{10,... | collective-permute-start | bytes 1544 | tf_op jit(solution)/shard_map/while/body/eval_jaxpr/ppermute | solution.py:10
  506.4 8.5 %collective-permute-start = (f32[4,32]{1,0:T(4,128)S(1)}, f32[4,32]{1,0:T(4,128)S(1)}, u32[]{:S(2)}, u32[]{:S(2)}) collective-permute-start(f32[4,32]{1,0:T(4,128)S(1)} %get-tuple-element.101), channel_id=1, source_target_pairs={{0,2},{1,3},{2,4},{3,5},{4,6},{5,7},{6,8},{7,9},{8,10},{9,11},{10,... | collective-permute-start | bytes 1544 | tf_op jit(solution)/shard_map/while/body/eval_jaxpr/ppermute | solution.py:10
  514.8 7.6 %collective-permute-start.1 = (f32[4,32]{1,0:T(4,128)S(1)}, f32[4,32]{1,0:T(4,128)S(1)}, u32[]{:S(2)}, u32[]{:S(2)}) collective-permute-start(f32[4,32]{1,0:T(4,128)S(1)} %add.124), channel_id=1, source_target_pairs={{0,32},{32,64},{64,96},{96,128},{128,160},{160,192},{192,224},{224... | collective-permute-start | bytes 1544 | tf_op jit(solution)/shard_map/while/body/eval_jaxpr/ppermute | solution.py:10
  522.4 8.5 %collective-permute-start = (f32[4,32]{1,0:T(4,128)S(1)}, f32[4,32]{1,0:T(4,128)S(1)}, u32[]{:S(2)}, u32[]{:S(2)}) collective-permute-start(f32[4,32]{1,0:T(4,128)S(1)} %get-tuple-element.101), channel_id=1, source_target_pairs={{0,2},{1,3},{2,4},{3,5},{4,6},{5,7},{6,8},{7,9},{8,10},{9,11},{10,... | collective-permute-start | bytes 1544 | tf_op jit(solution)/shard_map/while/body/eval_jaxpr/ppermute | solution.py:10
  538.5 8.5 %collective-permute-start = (f32[4,32]{1,0:T(4,128)S(1)}, f32[4,32]{1,0:T(4,128)S(1)}, u32[]{:S(2)}, u32[]{:S(2)}) collective-permute-start(f32[4,32]{1,0:T(4,128)S(1)} %get-tuple-element.101), channel_id=1, source_target_pairs={{0,2},{1,3},{2,4},{3,5},{4,6},{5,7},{6,8},{7,9},{8,10},{9,11},{10,... | collective-permute-start | bytes 1544 | tf_op jit(solution)/shard_map/while/body/eval_jaxpr/ppermute | solution.py:10
  554.5 8.5 %collective-permute-start = (f32[4,32]{1,0:T(4,128)S(1)}, f32[4,32]{1,0:T(4,128)S(1)}, u32[]{:S(2)}, u32[]{:S(2)}) collective-permute-start(f32[4,32]{1,0:T(4,128)S(1)} %get-tuple-element.101), channel_id=1, source_target_pairs={{0,2},{1,3},{2,4},{3,5},{4,6},{5,7},{6,8},{7,9},{8,10},{9,11},{10,... | collective-permute-start | bytes 1544 | tf_op jit(solution)/shard_map/while/body/eval_jaxpr/ppermute | solution.py:10
  570.6 8.5 %collective-permute-start = (f32[4,32]{1,0:T(4,128)S(1)}, f32[4,32]{1,0:T(4,128)S(1)}, u32[]{:S(2)}, u32[]{:S(2)}) collective-permute-start(f32[4,32]{1,0:T(4,128)S(1)} %get-tuple-element.101), channel_id=1, source_target_pairs={{0,2},{1,3},{2,4},{3,5},{4,6},{5,7},{6,8},{7,9},{8,10},{9,11},{10,... | collective-permute-start | bytes 1544 | tf_op jit(solution)/shard_map/while/body/eval_jaxpr/ppermute | solution.py:10
  586.6 8.5 %collective-permute-start = (f32[4,32]{1,0:T(4,128)S(1)}, f32[4,32]{1,0:T(4,128)S(1)}, u32[]{:S(2)}, u32[]{:S(2)}) collective-permute-start(f32[4,32]{1,0:T(4,128)S(1)} %get-tuple-element.101), channel_id=1, source_target_pairs={{0,2},{1,3},{2,4},{3,5},{4,6},{5,7},{6,8},{7,9},{8,10},{9,11},{10,... | collective-permute-start | bytes 1544 | tf_op jit(solution)/shard_map/while/body/eval_jaxpr/ppermute | solution.py:10
  602.7 8.5 %collective-permute-start = (f32[4,32]{1,0:T(4,128)S(1)}, f32[4,32]{1,0:T(4,128)S(1)}, u32[]{:S(2)}, u32[]{:S(2)}) collective-permute-start(f32[4,32]{1,0:T(4,128)S(1)} %get-tuple-element.101), channel_id=1, source_target_pairs={{0,2},{1,3},{2,4},{3,5},{4,6},{5,7},{6,8},{7,9},{8,10},{9,11},{10,... | collective-permute-start | bytes 1544 | tf_op jit(solution)/shard_map/while/body/eval_jaxpr/ppermute | solution.py:10
  618.8 8.5 %collective-permute-start = (f32[4,32]{1,0:T(4,128)S(1)}, f32[4,32]{1,0:T(4,128)S(1)}, u32[]{:S(2)}, u32[]{:S(2)}) collective-permute-start(f32[4,32]{1,0:T(4,128)S(1)} %get-tuple-element.101), channel_id=1, source_target_pairs={{0,2},{1,3},{2,4},{3,5},{4,6},{5,7},{6,8},{7,9},{8,10},{9,11},{10,... | collective-permute-start | bytes 1544 | tf_op jit(solution)/shard_map/while/body/eval_jaxpr/ppermute | solution.py:10
  627.2 7.6 %collective-permute-start.1 = (f32[4,32]{1,0:T(4,128)S(1)}, f32[4,32]{1,0:T(4,128)S(1)}, u32[]{:S(2)}, u32[]{:S(2)}) collective-permute-start(f32[4,32]{1,0:T(4,128)S(1)} %add.124), channel_id=1, source_target_pairs={{0,32},{32,64},{64,96},{96,128},{128,160},{160,192},{192,224},{224... | collective-permute-start | bytes 1544 | tf_op jit(solution)/shard_map/while/body/eval_jaxpr/ppermute | solution.py:10
  634.8 8.5 %collective-permute-start = (f32[4,32]{1,0:T(4,128)S(1)}, f32[4,32]{1,0:T(4,128)S(1)}, u32[]{:S(2)}, u32[]{:S(2)}) collective-permute-start(f32[4,32]{1,0:T(4,128)S(1)} %get-tuple-element.101), channel_id=1, source_target_pairs={{0,2},{1,3},{2,4},{3,5},{4,6},{5,7},{6,8},{7,9},{8,10},{9,11},{10,... | collective-permute-start | bytes 1544 | tf_op jit(solution)/shard_map/while/body/eval_jaxpr/ppermute | solution.py:10
  650.9 8.5 %collective-permute-start = (f32[4,32]{1,0:T(4,128)S(1)}, f32[4,32]{1,0:T(4,128)S(1)}, u32[]{:S(2)}, u32[]{:S(2)}) collective-permute-start(f32[4,32]{1,0:T(4,128)S(1)} %get-tuple-element.101), channel_id=1, source_target_pairs={{0,2},{1,3},{2,4},{3,5},{4,6},{5,7},{6,8},{7,9},{8,10},{9,11},{10,... | collective-permute-start | bytes 1544 | tf_op jit(solution)/shard_map/while/body/eval_jaxpr/ppermute | solution.py:10
  666.9 8.5 %collective-permute-start = (f32[4,32]{1,0:T(4,128)S(1)}, f32[4,32]{1,0:T(4,128)S(1)}, u32[]{:S(2)}, u32[]{:S(2)}) collective-permute-start(f32[4,32]{1,0:T(4,128)S(1)} %get-tuple-element.101), channel_id=1, source_target_pairs={{0,2},{1,3},{2,4},{3,5},{4,6},{5,7},{6,8},{7,9},{8,10},{9,11},{10,... | collective-permute-start | bytes 1544 | tf_op jit(solution)/shard_map/while/body/eval_jaxpr/ppermute | solution.py:10
  683.0 8.5 %collective-permute-start = (f32[4,32]{1,0:T(4,128)S(1)}, f32[4,32]{1,0:T(4,128)S(1)}, u32[]{:S(2)}, u32[]{:S(2)}) collective-permute-start(f32[4,32]{1,0:T(4,128)S(1)} %get-tuple-element.101), channel_id=1, source_target_pairs={{0,2},{1,3},{2,4},{3,5},{4,6},{5,7},{6,8},{7,9},{8,10},{9,11},{10,... | collective-permute-start | bytes 1544 | tf_op jit(solution)/shard_map/while/body/eval_jaxpr/ppermute | solution.py:10
  699.0 8.5 %collective-permute-start = (f32[4,32]{1,0:T(4,128)S(1)}, f32[4,32]{1,0:T(4,128)S(1)}, u32[]{:S(2)}, u32[]{:S(2)}) collective-permute-start(f32[4,32]{1,0:T(4,128)S(1)} %get-tuple-element.101), channel_id=1, source_target_pairs={{0,2},{1,3},{2,4},{3,5},{4,6},{5,7},{6,8},{7,9},{8,10},{9,11},{10,... | collective-permute-start | bytes 1544 | tf_op jit(solution)/shard_map/while/body/eval_jaxpr/ppermute | solution.py:10
  715.1 7.9 %collective-permute-start.4 = (f32[4,32]{1,0:T(4,128)S(1)}, f32[4,32]{1,0:T(4,128)S(1)}, u32[]{:S(2)}, u32[]{:S(2)}) collective-permute-start(f32[4,32]{1,0:T(4,128)S(1)} %get-tuple-element.58), channel_id=1, source_target_pairs={{0,1},{1,2},{2,3},{3,4},{4,5},{5,6},{6,7},{7,8},{8,9},{9,10},{10,1... | collective-permute-start | bytes 1544 | tf_op jit(solution)/shard_map/ppermute | solution.py:10
  717.0 8.5 %collective-permute-start.5 = (f32[4,32]{1,0:T(4,128)S(1)}, f32[4,32]{1,0:T(4,128)S(1)}, u32[]{:S(2)}, u32[]{:S(2)}) collective-permute-start(f32[4,32]{1,0:T(4,128)S(1)} %get-tuple-element.58), channel_id=1, source_target_pairs={{0,2},{1,3},{2,4},{3,5},{4,6},{5,7},{6,8},{7,9},{8,10},{9,11},{10,... | collective-permute-start | bytes 1544 | tf_op jit(solution)/shard_map/ppermute | solution.py:10
  (15 other events, 587.4 us)
Sparse Core Ops, SparseCore 0:
  9.4 155.3 all-gather.1
  176.3 279.7 all-reduce.14
where the time goes:
time: 738 us; the launch traced here: 735 us
  waiting for transfers between devices  622 us (84%)
  starting transfers between devices  80.9 us (11%)
  between operations  14.2 us (2%)
  matrix products  9 us (1%)
    unnamed x3, waiting for transfers between devices  278 us
    ppermute x34, waiting for transfers between devices, from_behind(): return lax.ppermute(block, axis, route)  186 us
    all_gather x1, waiting for transfers between devices, shards(): lax.all_gather(distrib, 'hrow', axis=1, tiled=True)  158 us
    ppermute x34, starting transfers between devices, from_behind(): return lax.ppermute(block, axis, route)  80.9 us
  transfers between devices with their start and end apart: 36, of which 35 were waited for; matrix products, arithmetic and copies ran while one was open for 0% of the time, Pallas kernels for 0%

commit v1 on v0

v1 whole, which is shorter than its diff:
```python
import functools

import jax
import jax.numpy as jnp
from jax import lax
from jax.experimental import pallas as pl
from jax.experimental.pallas import tpu as pltpu
from jax.sharding import PartitionSpec as P

PAIR = 2
RING = 8
COLS_X = 4
COLS_Y = 4
CORES = 2
ROWS = PAIR * RING
SPOTS = COLS_X * COLS_Y
MESH = pl.DeviceIdType.MESH


def kernel(
    e_hbm,
    d_hbm,
    direct_ref,
    out_ref,
    e_all,
    d_all,
    c_buf,
    x_buf,
    p_buf,
    slots,
    ends,
    carry,
    pad_direct,
    all_direct,
    swap_out,
    swap_in,
    local_sem,
    e_send,
    e_recv,
    d_send,
    d_recv,
    c_send,
    c_recv,
    p_send,
    p_recv,
    n_send,
    n_recv,
    s_send,
    s_recv,
):
    row = lax.axis_index("hrow")
    col = lax.axis_index("hcol")
    half = row // RING
    ring = row % RING
    core = col % CORES
    spot = col // CORES
    span = d_hbm.shape[0]
    dates = span // 2

    def ring_id(step):
        return (half * RING + lax.rem(ring + step + RING, RING), col)

    right, left = ring_id(1), ring_id(-1)
    mate = ((1 - half) * RING + ring, col)
    twin = (row, spot * CORES + (1 - core))

    def owner(block, band_half):
        return (band_half * RING + ring, (half * RING + block) * CORES + core)

    def signal(target):
        pl.semaphore_signal(barrier, inc=1, device_id=target, device_id_type=MESH)

    carry[...] = jnp.zeros_like(carry)
    pad_direct[...] = jnp.zeros_like(pad_direct)

    barrier = pltpu.get_barrier_semaphore()
    for target in (right, left, mate, twin):
        signal(target)
    source_half = spot // RING

    def greet_source(index, count):
        same = jnp.logical_and(source_half == half, index == spot)

        @pl.when(jnp.logical_not(same))
        def _():
            signal((source_half * RING + ring, index * CORES + core))

        return count + jnp.where(same, 0, 1)

    expected = lax.fori_loop(0, SPOTS, greet_source, jnp.int32(4))

    def link(down, side, way):
        other_row = row + way * down
        other_spot = spot + way * (down + side)
        valid = jnp.logical_and(other_row >= 0, other_row < ROWS)
        valid = jnp.logical_and(valid, jnp.logical_and(other_spot >= 0, other_spot < SPOTS))
        if side < 1:
            valid = jnp.logical_and(valid, down > 0)
        return valid, (other_row, other_spot * CORES + core)

    def greet_diagonal(down, count):
        for side in (-1, 0, 1):
            valid, upstream = link(down, side, -1)

            @pl.when(valid)
            def _():
                signal(upstream)

            valid, _ = link(down, side, 1)
            count = count + jnp.where(valid, 1, 0)
        return count

    expected = lax.fori_loop(0, ROWS, greet_diagonal, expected)

    own_e = pltpu.make_async_copy(e_hbm, e_all.at[half], local_sem.at[0])
    own_d = pltpu.make_async_copy(d_hbm, d_all.at[ring], local_sem.at[1])
    own_e.start()
    own_d.start()

    pl.semaphore_wait(barrier, expected)

    part = span // 4

    def piece(block, index):
        return d_all.at[block, pl.ds(index * part, part)]

    def d_copy(way, step, index, own):
        block = lax.rem(ring + (step if way else -step) + RING, RING)
        src = d_hbm.at[pl.ds(index * part, part)] if own else piece(block, index)
        return pltpu.make_async_remote_copy(
            src_ref=src,
            dst_ref=piece(block, index),
            send_sem=d_send.at[way, step, index],
            recv_sem=d_recv.at[way, step, index],
            device_id=left if way else right,
            device_id_type=MESH,
        )

    def d_arrival(way, step, index):
        block = lax.rem(ring + (step + 1 if way else -step - 1) + RING, RING)
        return pltpu.make_async_remote_copy(
            src_ref=piece(block, index),
            dst_ref=piece(block, index),
            send_sem=d_send.at[way, step, index],
            recv_sem=d_recv.at[way, step, index],
            device_id=left if way else right,
            device_id_type=MESH,
        )

    for index in range(4):
        for way in range(2):
            d_copy(way, 0, index, True).start()
    e_copy = pltpu.make_async_remote_copy(
        src_ref=e_hbm,
        dst_ref=e_all.at[half],
        send_sem=e_send,
        recv_sem=e_recv,
        device_id=mate,
        device_id_type=MESH,
    )
    e_copy.start()

    for shock in range(2):
        for outp in range(2):
            pad_direct[outp : outp + 1, shock * 64 : shock * 64 + 32] = direct_ref[shock, outp : outp + 1, :]
    own_direct = pad_direct[...]
    all_direct[0] = jnp.where(core == 0, own_direct, pltpu.roll(own_direct, 32, 1))
    direct_copy = pltpu.make_async_remote_copy(
        src_ref=all_direct.at[0],
        dst_ref=all_direct.at[1],
        send_sem=s_send.at[0],
        recv_sem=s_recv.at[0],
        device_id=twin,
        device_id_type=MESH,
    )
    direct_copy.start()

    def swap(turn):
        return pltpu.make_async_remote_copy(
            src_ref=c_buf.at[turn, :, 1 - core],
            dst_ref=x_buf.at[turn],
            send_sem=c_send.at[turn],
            recv_sem=c_recv.at[turn],
            device_id=twin,
            device_id_type=MESH,
        )

    def multiply(block, turn):
        product = lax.dot_general(
            e_all[...].reshape(2 * span, e_all.shape[2]),
            d_all[block],
            (((1,), (1,)), ((), ())),
            preferred_element_type=jnp.float32,
        )
        c_buf[turn] = product.reshape(2, 2, dates, span)
        swap(turn).start()

    def hand_over(block, band_half, turn):
        return pltpu.make_async_remote_copy(
            src_ref=p_buf.at[turn, band_half],
            dst_ref=slots.at[spot],
            send_sem=p_send.at[turn, band_half],
            recv_sem=p_recv.at[spot],
            device_id=owner(block, band_half),
            device_id_type=MESH,
        )

    def to_self(block, band_half):
        return jnp.logical_and(band_half == half, half * RING + block == spot)

    def deliver(block, turn):
        swap(turn).wait_recv()
        p_buf[turn] = c_buf[turn, :, core] + x_buf[turn]
        for band_half in range(2):
            mine = to_self(block, band_half)

            @pl.when(mine)
            def _():
                pltpu.make_async_copy(p_buf.at[turn, band_half], slots.at[spot], p_recv.at[spot]).start()

            @pl.when(jnp.logical_not(mine))
            def _():
                hand_over(block, band_half, turn).start()

    own_e.wait()
    own_d.wait()
    e_copy.wait_recv()
    multiply(ring, 0)
    deliver(ring, 0)

    def step_body(step, _):
        for index in range(4):
            for way in range(2):
                d_arrival(way, step - 1, index).wait_recv()
                if index // 2 == way:
                    d_copy(way, step, index, False).start()
                else:

                    @pl.when(step < 3)
                    def _():
                        d_copy(way, step, index, False).start()

        behind = lax.rem(ring - step + RING, RING)
        ahead = lax.rem(ring + step, RING)
        multiply(behind, 2 * step - 1)
        multiply(ahead, 2 * step)
        deliver(behind, 2 * step - 1)
        deliver(ahead, 2 * step)
        return 0

    lax.fori_loop(1, 4, step_body, 0)
    far = lax.rem(ring + 4, RING)
    for index in range(4):
        d_arrival(index // 2, 3, index).wait_recv()
    multiply(far, 7)
    deliver(far, 7)

    def arrived(index, _):
        pltpu.make_async_copy(slots.at[index], slots.at[index], p_recv.at[index]).wait()
        return 0

    lax.fori_loop(0, SPOTS, arrived, 0)
    total = slots[0]
    for index in range(1, SPOTS):
        total = total + slots[index]

    direct_copy.wait_recv()
    both_direct = all_direct[0] + all_direct[1]
    top = jnp.where(core == 0, both_direct[0:1], both_direct[1:2])
    top = jnp.where(row == 0, top, jnp.zeros_like(top))
    times = lax.broadcasted_iota(jnp.int32, (dates, span), 0)
    lanes = lax.broadcasted_iota(jnp.int32, (dates, span), 1)
    total = total + jnp.where(times == 0, top, 0.0)

    skewed = []
    for shock in range(2):
        tile = total if shock == 0 else pltpu.roll(total, 64, 1)
        tile = jnp.where(lanes < 64, tile, 0.0)
        for bit in range(6):
            moved = pltpu.roll(tile, 1 << bit, 1)
            tile = jnp.where(((63 - times) >> bit) & 1 == 1, moved, tile)
        skewed.append(tile)
        ends[shock : shock + 1, :] = jnp.sum(tile, axis=0, keepdims=True)

    def end_copy(down, side):
        valid, target = link(down, side, 1)
        return valid, pltpu.make_async_remote_copy(
            src_ref=ends,
            dst_ref=carry.at[down, side + 1],
            send_sem=n_send.at[down, side + 1],
            recv_sem=n_recv.at[down, side + 1],
            device_id=target,
            device_id_type=MESH,
        )

    def send_ends(down, _):
        for side in (-1, 0, 1):
            valid, copy = end_copy(down, side)

            @pl.when(valid)
            def _():
                copy.start()

        return 0

    lax.fori_loop(0, ROWS, send_ends, 0)

    summed = []
    for tile in skewed:
        for bit in range(6):
            offset = 1 << bit
            moved = pltpu.roll(tile, offset, 0)
            tile = tile + jnp.where(times >= offset, moved, 0.0)
        summed.append(tile)

    def receive_ends(down, _):
        for side in (-1, 0, 1):
            valid, _u = link(down, side, -1)

            @pl.when(valid)
            def _():
                end_copy(down, side)[1].wait_recv()

        return 0

    lax.fori_loop(0, ROWS, receive_ends, 0)
    incoming = jnp.sum(carry[...], axis=0)
    lane_row = lax.broadcasted_iota(jnp.int32, (2, span), 1)
    before = incoming[1]
    before = before + jnp.where(lane_row < 64, pltpu.roll(incoming[2], 64, 1), 0.0)
    before = before + jnp.where(lane_row >= 64, pltpu.roll(incoming[0], 64, 1), 0.0)

    finished = []
    for shock in range(2):
        tile = summed[shock] + before[shock : shock + 1]
        for bit in range(6):
            moved = pltpu.roll(tile, span - (1 << bit), 1)
            tile = jnp.where(((63 - times) >> bit) & 1 == 1, moved, tile)
        finished.append(tile)

    lower = finished
    upper = [pltpu.roll(tile, span - 32, 1) for tile in finished]
    mine = [jnp.where(core == 0, a, b) for a, b in zip(lower, upper)]
    theirs = [jnp.where(core == 0, b, a) for a, b in zip(lower, upper)]
    swap_out[...] = jnp.where(lanes < 32, theirs[0], pltpu.roll(theirs[1], 32, 1))
    last = pltpu.make_async_remote_copy(
        src_ref=swap_out,
        dst_ref=swap_in,
        send_sem=s_send.at[1],
        recv_sem=s_recv.at[1],
        device_id=twin,
        device_id_type=MESH,
    )
    last.start()
    for shock in range(2):
        out_ref[core, shock] = mine[shock][:, :32]

    def left_d(step, _):
        for index in range(4):
            for way in range(2):
                if index // 2 == way:
                    d_copy(way, step, index, False).wait_send()
                else:

                    @pl.when(step < 3)
                    def _():
                        d_copy(way, step, index, False).wait_send()

        return 0

    lax.fori_loop(0, 4, left_d, 0)
    e_copy.wait_send()
    direct_copy.wait_send()

    def left_p(turn, _):
        swap(turn).wait_send()
        away = (turn + 1) // 2
        block = lax.rem(ring + jnp.where(turn % 2 == 1, -away, away) + RING, RING)
        for band_half in range(2):

            @pl.when(jnp.logical_not(to_self(block, band_half)))
            def _():
                hand_over(block, band_half, turn).wait_send()

        return 0

    lax.fori_loop(0, RING, left_p, 0)

    def left_n(down, _):
        for side in (-1, 0, 1):
            valid, copy = end_copy(down, side)

            @pl.when(valid)
            def _():
                copy.wait_send()

        return 0

    lax.fori_loop(0, ROWS, left_n, 0)
    last.wait()
    received = swap_in[...]
    out_ref[1 - core, 0] = received[:, :32]
    out_ref[1 - core, 1] = pltpu.roll(received, span - 32, 1)[:, :32]


def blocks(expect, distrib, direct):
    outs, dates, points = expect.shape
    span = outs * dates
    dma = pltpu.SemaphoreType.DMA
    return pl.pallas_call(
        kernel,
        out_shape=jax.ShapeDtypeStruct((2, 2, dates, dates // 2), jnp.float32),
        in_specs=[
            pl.BlockSpec(memory_space=pl.ANY),
            pl.BlockSpec(memory_space=pl.ANY),
            pl.BlockSpec(memory_space=pltpu.VMEM),
        ],
        out_specs=pl.BlockSpec(memory_space=pltpu.VMEM),
        scratch_shapes=[
            pltpu.VMEM((PAIR, span, points), jnp.bfloat16),
            pltpu.VMEM((RING, span, points), jnp.bfloat16),
            pltpu.VMEM((RING, PAIR, 2, dates, span), jnp.float32),
            pltpu.VMEM((RING, PAIR, dates, span), jnp.float32),
            pltpu.VMEM((RING, PAIR, dates, span), jnp.float32),
            pltpu.VMEM((SPOTS, dates, span), jnp.float32),
            pltpu.VMEM((2, span), jnp.float32),
            pltpu.VMEM((ROWS, 3, 2, span), jnp.float32),
            pltpu.VMEM((8, span), jnp.float32),
            pltpu.VMEM((2, 8, span), jnp.float32),
            pltpu.VMEM((dates, span), jnp.float32),
            pltpu.VMEM((dates, span), jnp.float32),
            dma((2,)),
            dma,
            dma,
            dma((2, 4, 4)),
            dma((2, 4, 4)),
            dma((RING,)),
            dma((RING,)),
            dma((RING, PAIR)),
            dma((SPOTS,)),
            dma((ROWS, 3)),
            dma((ROWS, 3)),
            dma((2,)),
            dma((2,)),
        ],
        compiler_params=pltpu.CompilerParams(
            collective_id=0, has_side_effects=True, vmem_limit_bytes=40 * 1024 * 1024
        ),
    )(expect.reshape(span, points), distrib.reshape(span, points), direct)


def shards(expect, distrib, direct, pair_index):
    products = blocks(expect, distrib, direct)
    shock = pair_index[:, 0][:, None, None]
    outp = pair_index[:, 1][:, None, None]
    first = jnp.where(shock == 0, products[0, 0], products[0, 1])
    second = jnp.where(shock == 0, products[1, 0], products[1, 1])
    return jnp.where(outp == 0, first, second)


def solution(mesh):
    placed = (P(None, "hrow", "hcol"), P(None, "hrow", "hcol"), P(None, None, "hcol"), P())
    return jax.shard_map(
        shards, mesh=mesh, in_specs=placed, out_specs=P(None, "hrow", "hcol"), check_vma=False
    )
```

time: 738 us -> 108 us (0.15)
  the two profiles are of different devices: /device:TPU:14 before, /device:TPU:15 now
where the time goes in v1:
time: 108 us; the launch traced here: 107 us
  Pallas kernels  103 us (95%)
  local copies, waits for them, and re-layouts  3.89 us (4%)
    pallas_call x1, Pallas kernels, blocks(): pl.pallas_call(kernel, out_shape=jax.ShapeDtypeStruct((2, 2, dates, dates...  103 us
    unnamed x8, local copies, waits for them, and re-layouts  3.59 us

profile of v1, /device:TPU:15, one launch (start us, length us, event | category | flops | bytes accessed | tf_op | source)
XLA Modules:
  0.0 107.5 jit_solution(6136748320586926061)
XLA Ops:
  0.0 0.0 copy-start.2
  0.0 0.7 copy-done.2
  0.7 0.0 copy-start
  0.7 1.1 %copy-done = bf16[2,64,3200]{2,1,0:T(8,128)(2,1)S(1)} copy-done((bf16[2,64,3200]{2,1,0:T(8,128)(2,1)S(1)}, bf16[2,64,3200]{2,1,0:T(8,128)(2,1)}, u32[]{:S(2)}) %copy-start) | copy-done | bytes 819224
  1.8 0.0 copy-start.1
  1.8 1.1 %copy-done.1 = bf16[2,64,3200]{2,1,0:T(8,128)(2,1)S(1)} copy-done((bf16[2,64,3200]{2,1,0:T(8,128)(2,1)S(1)}, bf16[2,64,3200]{2,1,0:T(8,128)(2,1)}, u32[]{:S(2)}) %copy-start.1) | copy-done | bytes 819224
  3.0 102.8 %shard_map.46 = f32[2,2,64,32]{3,2,1,0:T(8,128)S(1)} custom-call(bf16[128,3200]{1,0:T(8,128)(2,1)S(1)} %bitcast.14, bf16[128,3200]{1,0:T(8,128)(2,1)S(1)} %bitcast.15, f32[2,2,32]{2,1,0:T(2,128)S(1)} %copy-done.2), custom_call_target="tpu_custom_call" | custom-call | tf_op jit(solution)/shard_map/pallas_call | solution.py:410
  105.8 0.1 copy.5
  105.9 0.1 copy.6
  106.0 0.1 copy.7
  106.1 0.0 copy-start.3
  106.1 0.1 copy.8
  106.1 0.6 copy-done.3
  106.8 0.7 select_select_fusion
  (2 shorter events, 0.0 us)
Async XLA Ops:
  0.0 0.7 copy-start.2
  0.7 1.1 %copy-start = (bf16[2,64,3200]{2,1,0:T(8,128)(2,1)S(1)}, bf16[2,64,3200]{2,1,0:T(8,128)(2,1)}, u32[]{:S(2)}) copy-start(bf16[2,64,3200]{2,1,0:T(8,128)(2,1)} %param.4) | copy-start | bytes 2457604
  1.8 1.1 %copy-start.1 = (bf16[2,64,3200]{2,1,0:T(8,128)(2,1)S(1)}, bf16[2,64,3200]{2,1,0:T(8,128)(2,1)}, u32[]{:S(2)}) copy-start(bf16[2,64,3200]{2,1,0:T(8,128)(2,1)} %param.5) | copy-start | bytes 2457604
  106.1 0.7 copy-start.3

commit v2 on v1

--- a/solution.py
+++ b/solution.py
@@ -1,5 +1,3 @@
-import functools
-
 import jax
 import jax.numpy as jnp
 from jax import lax
@@ -47,6 +45,7 @@
     n_recv,
     s_send,
     s_recv,
+    word_sem,
 ):
     row = lax.axis_index("hrow")
     col = lax.axis_index("hcol")
@@ -64,6 +63,12 @@
     mate = ((1 - half) * RING + ring, col)
     twin = (row, spot * CORES + (1 - core))
 
+    def x_peer(step):
+        return (row, lax.rem(spot + COLS_Y * step, SPOTS) * CORES + core)
+
+    def y_peer(step):
+        return (row, (spot // COLS_Y * COLS_Y + lax.rem(spot + step, COLS_Y)) * CORES + core)
+
     def owner(block, band_half):
         return (band_half * RING + ring, (half * RING + block) * CORES + core)
 
@@ -76,6 +81,9 @@
     barrier = pltpu.get_barrier_semaphore()
     for target in (right, left, mate, twin):
         signal(target)
+    for step in (1, 2, 3):
+        signal(x_peer(step))
+        signal(y_peer(step))
     source_half = spot // RING
 
     def greet_source(index, count):
@@ -87,7 +95,7 @@
 
         return count + jnp.where(same, 0, 1)
 
-    expected = lax.fori_loop(0, SPOTS, greet_source, jnp.int32(4))
+    expected = lax.fori_loop(0, SPOTS, greet_source, jnp.int32(10))
 
     def link(down, side, way):
         other_row = row + way * down
@@ -97,20 +105,6 @@
         if side < 1:
             valid = jnp.logical_and(valid, down > 0)
         return valid, (other_row, other_spot * CORES + core)
-
-    def greet_diagonal(down, count):
-        for side in (-1, 0, 1):
-            valid, upstream = link(down, side, -1)
-
-            @pl.when(valid)
-            def _():
-                signal(upstream)
-
-            valid, _ = link(down, side, 1)
-            count = count + jnp.where(valid, 1, 0)
-        return count
-
-    expected = lax.fori_loop(0, ROWS, greet_diagonal, expected)
 
     own_e = pltpu.make_async_copy(e_hbm, e_all.at[half], local_sem.at[0])
     own_d = pltpu.make_async_copy(d_hbm, d_all.at[ring], local_sem.at[1])
@@ -222,12 +216,6 @@
             def _():
                 hand_over(block, band_half, turn).start()
 
-    own_e.wait()
-    own_d.wait()
-    e_copy.wait_recv()
-    multiply(ring, 0)
-    deliver(ring, 0)
-
     def step_body(step, _):
         for index in range(4):
             for way in range(2):
@@ -240,6 +228,14 @@
                     def _():
                         d_copy(way, step, index, False).start()
 
+        @pl.when(step == 1)
+        def _():
+            own_e.wait()
+            own_d.wait()
+            e_copy.wait_recv()
+            multiply(ring, 0)
+            deliver(ring, 0)
+
         behind = lax.rem(ring - step + RING, RING)
         ahead = lax.rem(ring + step, RING)
         multiply(behind, 2 * step - 1)
@@ -252,8 +248,15 @@
     far = lax.rem(ring + 4, RING)
     for index in range(4):
         d_arrival(index // 2, 3, index).wait_recv()
+    pl.semaphore_signal(word_sem.at[0], inc=1, device_id=mate, device_id_type=MESH)
     multiply(far, 7)
+    pl.semaphore_wait(word_sem.at[0], 1)
+    for step in (1, 2, 3):
+        pl.semaphore_signal(word_sem.at[1], inc=1, device_id=x_peer(step), device_id_type=MESH)
     deliver(far, 7)
+    pl.semaphore_wait(word_sem.at[1], 3)
+    for step in (1, 2, 3):
+        pl.semaphore_signal(word_sem.at[2], inc=1, device_id=y_peer(step), device_id_type=MESH)
 
     def arrived(index, _):
         pltpu.make_async_copy(slots.at[index], slots.at[index], p_recv.at[index]).wait()
@@ -303,6 +306,7 @@
 
         return 0
 
+    pl.semaphore_wait(word_sem.at[2], 3)
     lax.fori_loop(0, ROWS, send_ends, 0)
 
     summed = []
@@ -442,9 +446,10 @@
             dma((ROWS, 3)),
             dma((2,)),
             dma((2,)),
+            pltpu.SemaphoreType.REGULAR((3,)),
         ],
         compiler_params=pltpu.CompilerParams(
-            collective_id=0, has_side_effects=True, vmem_limit_bytes=40 * 1024 * 1024
+            collective_id=0, has_side_effects=True, vmem_limit_bytes=58 * 1024 * 1024
         ),
     )(expect.reshape(span, points), distrib.reshape(span, points), direct)
 

time: 108 us -> 101 us (0.935)
  the two profiles are of different devices: /device:TPU:15 before, /device:TPU:11 now
where the time goes in v2:
time: 101 us
  Pallas kernels  98.7 us (98%)
  local copies, waits for them, and re-layouts  1.73 us (2%)
    pallas_call x1, Pallas kernels, blocks(): pl.pallas_call(kernel, out_shape=jax.ShapeDtypeStruct((2, 2, dates, dates...  98.7 us

profile of v2, /device:TPU:11, one launch (start us, length us, event | category | flops | bytes accessed | tf_op | source)
XLA Modules:
  0.0 101.2 jit_solution(16522388416526846851)
XLA Ops:
  0.0 98.7 %shard_map.46 = f32[2,2,64,32]{3,2,1,0:T(8,128)} custom-call(bf16[128,3200]{1,0:T(8,128)(2,1)} %bitcast.14, bf16[128,3200]{1,0:T(8,128)(2,1)} %bitcast.15, f32[2,2,32]{2,1,0:T(2,128)} %direct_ref.1), custom_call_target="tpu_custom_call" | custom-call | tf_op jit(solution)/shard_map/pallas_call | solution.py:414
  98.8 0.8 slice_bitcast_fusion.3
  99.6 0.1 copy.5
  99.6 0.1 copy.6
  99.7 0.1 copy.7
  99.8 0.0 copy-start
  99.8 0.1 copy.8
  99.9 0.6 copy-done
  100.5 0.7 select_select_fusion
  (1 shorter events, 0.0 us)
Async XLA Ops:
  99.8 0.7 copy-start

commit v3 on v2

--- a/solution.py
+++ b/solution.py
@@ -18,7 +18,7 @@
 def kernel(
     e_hbm,
     d_hbm,
-    direct_ref,
+    direct_hbm,
     out_ref,
     e_all,
     d_all,
@@ -28,6 +28,7 @@
     slots,
     ends,
     carry,
+    direct_ref,
     pad_direct,
     all_direct,
     swap_out,
@@ -108,6 +109,8 @@
 
     own_e = pltpu.make_async_copy(e_hbm, e_all.at[half], local_sem.at[0])
     own_d = pltpu.make_async_copy(d_hbm, d_all.at[ring], local_sem.at[1])
+    own_direct = pltpu.make_async_copy(direct_hbm, direct_ref, local_sem.at[2])
+    own_direct.start()
     own_e.start()
     own_d.start()
 
@@ -154,11 +157,12 @@
     )
     e_copy.start()
 
+    own_direct.wait()
     for shock in range(2):
         for outp in range(2):
             pad_direct[outp : outp + 1, shock * 64 : shock * 64 + 32] = direct_ref[shock, outp : outp + 1, :]
-    own_direct = pad_direct[...]
-    all_direct[0] = jnp.where(core == 0, own_direct, pltpu.roll(own_direct, 32, 1))
+    raw_direct = pad_direct[...]
+    all_direct[0] = jnp.where(core == 0, raw_direct, pltpu.roll(raw_direct, 32, 1))
     direct_copy = pltpu.make_async_remote_copy(
         src_ref=all_direct.at[0],
         dst_ref=all_direct.at[1],
@@ -216,7 +220,7 @@
             def _():
                 hand_over(block, band_half, turn).start()
 
-    def step_body(step, _):
+    def pass_on(step):
         for index in range(4):
             for way in range(2):
                 d_arrival(way, step - 1, index).wait_recv()
@@ -228,32 +232,48 @@
                     def _():
                         d_copy(way, step, index, False).start()
 
-        @pl.when(step == 1)
+    def block_at(turn):
+        away = (turn + 1) // 2
+        return lax.rem(ring + jnp.where(turn % 2 == 1, -away, away) + RING, RING)
+
+    def turn_body(turn, _):
+        opens_step = jnp.logical_or(turn == 0, jnp.logical_or(turn == 3, turn == 5))
+
+        @pl.when(opens_step)
+        def _():
+            pass_on(jnp.where(turn == 0, 1, (turn + 1) // 2))
+
+        @pl.when(turn == 0)
         def _():
             own_e.wait()
             own_d.wait()
             e_copy.wait_recv()
-            multiply(ring, 0)
-            deliver(ring, 0)
-
-        behind = lax.rem(ring - step + RING, RING)
-        ahead = lax.rem(ring + step, RING)
-        multiply(behind, 2 * step - 1)
-        multiply(ahead, 2 * step)
-        deliver(behind, 2 * step - 1)
-        deliver(ahead, 2 * step)
-        return 0
-
-    lax.fori_loop(1, 4, step_body, 0)
-    far = lax.rem(ring + 4, RING)
-    for index in range(4):
-        d_arrival(index // 2, 3, index).wait_recv()
-    pl.semaphore_signal(word_sem.at[0], inc=1, device_id=mate, device_id_type=MESH)
-    multiply(far, 7)
-    pl.semaphore_wait(word_sem.at[0], 1)
-    for step in (1, 2, 3):
-        pl.semaphore_signal(word_sem.at[1], inc=1, device_id=x_peer(step), device_id_type=MESH)
-    deliver(far, 7)
+
+        @pl.when(turn == 7)
+        def _():
+            for index in range(4):
+                d_arrival(index // 2, 3, index).wait_recv()
+            pl.semaphore_signal(word_sem.at[0], inc=1, device_id=mate, device_id_type=MESH)
+
+        multiply(block_at(turn), turn)
+
+        @pl.when(turn == 7)
+        def _():
+            pl.semaphore_wait(word_sem.at[0], 1)
+            for step in (1, 2, 3):
+                pl.semaphore_signal(word_sem.at[1], inc=1, device_id=x_peer(step), device_id_type=MESH)
+
+        @pl.when(jnp.logical_and(turn % 2 == 0, turn > 0))
+        def _():
+            deliver(block_at(turn - 1), turn - 1)
+
+        @pl.when(jnp.logical_or(turn % 2 == 0, turn == 7))
+        def _():
+            deliver(block_at(turn), turn)
+
+        return 0
+
+    lax.fori_loop(0, RING, turn_body, 0)
     pl.semaphore_wait(word_sem.at[1], 3)
     for step in (1, 2, 3):
         pl.semaphore_signal(word_sem.at[2], inc=1, device_id=y_peer(step), device_id_type=MESH)
@@ -316,6 +336,36 @@
             moved = pltpu.roll(tile, offset, 0)
             tile = tile + jnp.where(times >= offset, moved, 0.0)
         summed.append(tile)
+
+    def left_d(step, _):
+        for index in range(4):
+            for way in range(2):
+                if index // 2 == way:
+                    d_copy(way, step, index, False).wait_send()
+                else:
+
+                    @pl.when(step < 3)
+                    def _():
+                        d_copy(way, step, index, False).wait_send()
+
+        return 0
+
+    lax.fori_loop(0, 4, left_d, 0)
+    e_copy.wait_send()
+    direct_copy.wait_send()
+
+    def left_p(turn, _):
+        swap(turn).wait_send()
+        block = block_at(turn)
+        for band_half in range(2):
+
+            @pl.when(jnp.logical_not(to_self(block, band_half)))
+            def _():
+                hand_over(block, band_half, turn).wait_send()
+
+        return 0
+
+    lax.fori_loop(0, RING, left_p, 0)
 
     def receive_ends(down, _):
         for side in (-1, 0, 1):
@@ -359,37 +409,6 @@
     for shock in range(2):
         out_ref[core, shock] = mine[shock][:, :32]
 
-    def left_d(step, _):
-        for index in range(4):
-            for way in range(2):
-                if index // 2 == way:
-                    d_copy(way, step, index, False).wait_send()
-                else:
-
-                    @pl.when(step < 3)
-                    def _():
-                        d_copy(way, step, index, False).wait_send()
-
-        return 0
-
-    lax.fori_loop(0, 4, left_d, 0)
-    e_copy.wait_send()
-    direct_copy.wait_send()
-
-    def left_p(turn, _):
-        swap(turn).wait_send()
-        away = (turn + 1) // 2
-        block = lax.rem(ring + jnp.where(turn % 2 == 1, -away, away) + RING, RING)
-        for band_half in range(2):
-
-            @pl.when(jnp.logical_not(to_self(block, band_half)))
-            def _():
-                hand_over(block, band_half, turn).wait_send()
-
-        return 0
-
-    lax.fori_loop(0, RING, left_p, 0)
-
     def left_n(down, _):
         for side in (-1, 0, 1):
             valid, copy = end_copy(down, side)
@@ -417,7 +436,7 @@
         in_specs=[
             pl.BlockSpec(memory_space=pl.ANY),
             pl.BlockSpec(memory_space=pl.ANY),
-            pl.BlockSpec(memory_space=pltpu.VMEM),
+            pl.BlockSpec(memory_space=pl.ANY),
         ],
         out_specs=pl.BlockSpec(memory_space=pltpu.VMEM),
         scratch_shapes=[
@@ -429,11 +448,12 @@
             pltpu.VMEM((SPOTS, dates, span), jnp.float32),
             pltpu.VMEM((2, span), jnp.float32),
             pltpu.VMEM((ROWS, 3, 2, span), jnp.float32),
+            pltpu.VMEM((2, 2, dates // 2), jnp.float32),
             pltpu.VMEM((8, span), jnp.float32),
             pltpu.VMEM((2, 8, span), jnp.float32),
             pltpu.VMEM((dates, span), jnp.float32),
             pltpu.VMEM((dates, span), jnp.float32),
-            dma((2,)),
+            dma((3,)),
             dma,
             dma,
             dma((2, 4, 4)),

time: 101 us -> 101 us (level)
  no operation moved by 1% of the time
where the time goes in v3:
time: 101 us
  Pallas kernels  98.1 us (97%)
  local copies, waits for them, and re-layouts  1.73 us (2%)
    pallas_call x1, Pallas kernels, blocks(): pl.pallas_call(kernel, out_shape=jax.ShapeDtypeStruct((2, 2, dates, dates...  98.1 us

profile of v3, /device:TPU:11, one launch (start us, length us, event | category | flops | bytes accessed | tf_op | source)
XLA Modules:
  0.0 100.5 jit_solution(9669075835491136867)
XLA Ops:
  0.0 98.1 %shard_map.46 = f32[2,2,64,32]{3,2,1,0:T(8,128)} custom-call(bf16[128,3200]{1,0:T(8,128)(2,1)} %bitcast.14, bf16[128,3200]{1,0:T(8,128)(2,1)} %bitcast.15, f32[2,2,32]{2,1,0:T(2,128)} %direct_hbm.1), custom_call_target="tpu_custom_call" | custom-call | tf_op jit(solution)/shard_map/pallas_call | solution.py:433
  98.1 0.8 slice_bitcast_fusion.3
  98.9 0.1 copy.5
  99.0 0.1 copy.6
  99.1 0.1 copy.7
  99.1 0.0 copy-start
  99.1 0.1 copy.8
  99.2 0.6 copy-done
  99.8 0.7 select_select_fusion
  (1 shorter events, 0.0 us)
Async XLA Ops:
  99.1 0.7 copy-start

commit v4 on v3

--- a/solution.py
+++ b/solution.py
@@ -67,6 +67,9 @@
     def x_peer(step):
         return (row, lax.rem(spot + COLS_Y * step, SPOTS) * CORES + core)
 
+    def mate_x_peer(step):
+        return (mate[0], x_peer(step)[1])
+
     def y_peer(step):
         return (row, (spot // COLS_Y * COLS_Y + lax.rem(spot + step, COLS_Y)) * CORES + core)
 
@@ -75,6 +78,7 @@
 
     def signal(target):
         pl.semaphore_signal(barrier, inc=1, device_id=target, device_id_type=MESH)
+
 
     carry[...] = jnp.zeros_like(carry)
     pad_direct[...] = jnp.zeros_like(pad_direct)
@@ -85,6 +89,7 @@
     for step in (1, 2, 3):
         signal(x_peer(step))
         signal(y_peer(step))
+        signal(mate_x_peer(step))
     source_half = spot // RING
 
     def greet_source(index, count):
@@ -96,7 +101,7 @@
 
         return count + jnp.where(same, 0, 1)
 
-    expected = lax.fori_loop(0, SPOTS, greet_source, jnp.int32(10))
+    expected = lax.fori_loop(0, SPOTS, greet_source, jnp.int32(13))
 
     def link(down, side, way):
         other_row = row + way * down
@@ -253,16 +258,11 @@
         def _():
             for index in range(4):
                 d_arrival(index // 2, 3, index).wait_recv()
-            pl.semaphore_signal(word_sem.at[0], inc=1, device_id=mate, device_id_type=MESH)
+            for target in [mate] + [x_peer(step) for step in (1, 2, 3)] + [mate_x_peer(step) for step in (1, 2, 3)]:
+                pl.semaphore_signal(word_sem.at[0], inc=1, device_id=target, device_id_type=MESH)
 
         multiply(block_at(turn), turn)
 
-        @pl.when(turn == 7)
-        def _():
-            pl.semaphore_wait(word_sem.at[0], 1)
-            for step in (1, 2, 3):
-                pl.semaphore_signal(word_sem.at[1], inc=1, device_id=x_peer(step), device_id_type=MESH)
-
         @pl.when(jnp.logical_and(turn % 2 == 0, turn > 0))
         def _():
             deliver(block_at(turn - 1), turn - 1)
@@ -274,9 +274,9 @@
         return 0
 
     lax.fori_loop(0, RING, turn_body, 0)
-    pl.semaphore_wait(word_sem.at[1], 3)
+    pl.semaphore_wait(word_sem.at[0], 7)
     for step in (1, 2, 3):
-        pl.semaphore_signal(word_sem.at[2], inc=1, device_id=y_peer(step), device_id_type=MESH)
+        pl.semaphore_signal(word_sem.at[1], inc=1, device_id=y_peer(step), device_id_type=MESH)
 
     def arrived(index, _):
         pltpu.make_async_copy(slots.at[index], slots.at[index], p_recv.at[index]).wait()
@@ -299,9 +299,15 @@
     for shock in range(2):
         tile = total if shock == 0 else pltpu.roll(total, 64, 1)
         tile = jnp.where(lanes < 64, tile, 0.0)
-        for bit in range(6):
+        for bit in range(3):
             moved = pltpu.roll(tile, 1 << bit, 1)
             tile = jnp.where(((63 - times) >> bit) & 1 == 1, moved, tile)
+        groups = [tile[start : start + 8] for start in range(0, dates, 8)]
+        groups = [
+            pltpu.roll(group, dates - 8 - 8 * index, 1) if index < RING - 1 else group
+            for index, group in enumerate(groups)
+        ]
+        tile = jnp.concatenate(groups, axis=0)
         skewed.append(tile)
         ends[shock : shock + 1, :] = jnp.sum(tile, axis=0, keepdims=True)
 
@@ -316,9 +322,9 @@
             device_id_type=MESH,
         )
 
-    def send_ends(down, _):
+    def send_ends(near, _):
         for side in (-1, 0, 1):
-            valid, copy = end_copy(down, side)
+            valid, copy = end_copy(ROWS - 1 - near, side)
 
             @pl.when(valid)
             def _():
@@ -326,7 +332,7 @@
 
         return 0
 
-    pl.semaphore_wait(word_sem.at[2], 3)
+    pl.semaphore_wait(word_sem.at[1], 3)
     lax.fori_loop(0, ROWS, send_ends, 0)
 
     summed = []
@@ -387,9 +393,7 @@
     finished = []
     for shock in range(2):
         tile = summed[shock] + before[shock : shock + 1]
-        for bit in range(6):
-            moved = pltpu.roll(tile, span - (1 << bit), 1)
-            tile = jnp.where(((63 - times) >> bit) & 1 == 1, moved, tile)
+        tile = pltpu.roll(tile, span - 63, 1, stride=1, stride_axis=0)
         finished.append(tile)
 
     lower = finished
@@ -466,7 +470,7 @@
             dma((ROWS, 3)),
             dma((2,)),
             dma((2,)),
-            pltpu.SemaphoreType.REGULAR((3,)),
+            pltpu.SemaphoreType.REGULAR((2,)),
         ],
         compiler_params=pltpu.CompilerParams(
             collective_id=0, has_side_effects=True, vmem_limit_bytes=58 * 1024 * 1024

time: 101 us -> 100 us (0.990)
  no operation moved by 1% of the time
where the time goes in v4:
time: 100 us; the launch traced here: 99.8 us
  Pallas kernels  97.4 us (97%)
  local copies, waits for them, and re-layouts  1.73 us (2%)
    pallas_call x1, Pallas kernels, blocks(): pl.pallas_call(kernel, out_shape=jax.ShapeDtypeStruct((2, 2, dates, dates...  97.4 us

profile of v4, /device:TPU:11, one launch (start us, length us, event | category | flops | bytes accessed | tf_op | source)
XLA Modules:
  0.0 99.8 jit_solution(9975965687116008181)
XLA Ops:
  0.0 97.4 %shard_map.46 = f32[2,2,64,32]{3,2,1,0:T(8,128)} custom-call(bf16[128,3200]{1,0:T(8,128)(2,1)} %bitcast.14, bf16[128,3200]{1,0:T(8,128)(2,1)} %bitcast.15, f32[2,2,32]{2,1,0:T(2,128)} %direct_hbm.1), custom_call_target="tpu_custom_call" | custom-call | tf_op jit(solution)/shard_map/pallas_call | solution.py:437
  97.4 0.8 slice_bitcast_fusion.3
  98.2 0.1 copy.5
  98.3 0.1 copy.6
  98.4 0.1 copy.7
  98.4 0.0 copy-start
  98.4 0.1 copy.8
  98.5 0.6 copy-done
  99.1 0.7 select_select_fusion
  (1 shorter events, 0.0 us)
Async XLA Ops:
  98.4 0.7 copy-start

commit v5 on v4

--- a/solution.py
+++ b/solution.py
@@ -189,14 +189,17 @@
         )
 
     def multiply(block, turn):
-        product = lax.dot_general(
-            e_all[...].reshape(2 * span, e_all.shape[2]),
-            d_all[block],
-            (((1,), (1,)), ((), ())),
-            preferred_element_type=jnp.float32,
-        )
-        c_buf[turn] = product.reshape(2, 2, dates, span)
-        swap(turn).start()
+        for outp in (1 - core, core):
+            rows = e_all[:, pl.ds(pl.multiple_of(outp * dates, dates), dates)]
+            product = lax.dot_general(
+                rows.reshape(span, e_all.shape[2]),
+                d_all[block],
+                (((1,), (1,)), ((), ())),
+                preferred_element_type=jnp.float32,
+            )
+            c_buf[turn, :, outp] = product.reshape(2, dates, span)
+            if outp is not core:
+                swap(turn).start()
 
     def hand_over(block, band_half, turn):
         return pltpu.make_async_remote_copy(

time: 100 us -> 101 us (1.010)
  no operation moved by 1% of the time
where the time goes in v5:
time: 101 us
  Pallas kernels  98.1 us (97%)
  local copies, waits for them, and re-layouts  1.73 us (2%)
    pallas_call x1, Pallas kernels, blocks(): pl.pallas_call(kernel, out_shape=jax.ShapeDtypeStruct((2, 2, dates, dates...  98.1 us

profile of v5, /device:TPU:11, one launch (start us, length us, event | category | flops | bytes accessed | tf_op | source)
XLA Modules:
  0.0 100.6 jit_solution(15324205461188104717)
XLA Ops:
  0.0 98.1 %shard_map.46 = f32[2,2,64,32]{3,2,1,0:T(8,128)} custom-call(bf16[128,3200]{1,0:T(8,128)(2,1)} %bitcast.14, bf16[128,3200]{1,0:T(8,128)(2,1)} %bitcast.15, f32[2,2,32]{2,1,0:T(2,128)} %direct_hbm.1), custom_call_target="tpu_custom_call" | custom-call | tf_op jit(solution)/shard_map/pallas_call | solution.py:440
  98.2 0.8 slice_bitcast_fusion.3
  99.0 0.1 copy.5
  99.0 0.1 copy.6
  99.1 0.1 copy.7
  99.2 0.0 copy-start
  99.2 0.1 copy.8
  99.3 0.6 copy-done
  99.9 0.7 select_select_fusion
  (1 shorter events, 0.0 us)
Async XLA Ops:
  99.2 0.7 copy-start
